TPU v7x, 256 devices: a whole 4x4x8 slice. The times are simulated.
256 devices in a mesh: row: 32 (over y, z), col: 8 (over x, core).
Axes of the slice: x: 4, y: 4, z: 8, core: 2. Of those that a mesh axis runs over, the one named last changes fastest.
Arguments:
- acts: bfloat16 [6144, 28672], P('col', 'row'), may hold values from -12 to 12
- out_grad: bfloat16 [6144, 8192], P('row', 'col'), may hold values from -12 to 12
- lengths: int32 [8], replicated, may hold values from 1 to 768, 4800 in all
Outputs:
- weight_grad: bfloat16 [28672, 8192], P('row', 'col')
- norms: float32 [8], replicated
All inputs are finite; a program needn't handle non-finite values.
Results may differ from a plain program's by a relative error of at most 0.0013.
Values may be sent and summed in bfloat16 or wider, within the bound.
No kernel may reach another device: no remote copies, remote signals or barrier semaphores. Data moves between devices by JAX's collectives and lax.ppermute only.
A program may use at most 128 MiB of HBM per device.

v0:
```python
import jax
import jax.numpy as jnp
from jax import lax
from jax.sharding import PartitionSpec as P

FF = 28672
D = 8192


def exchange_sum(value, axis, shifts):
    size = lax.axis_size(axis)
    parts = [value]
    for shift in shifts:
        parts.append(lax.ppermute(value, axis, [(i, i ^ shift) for i in range(size)]))
    while len(parts) > 1:
        parts = [parts[i] + parts[i + 1] for i in range(0, len(parts), 2)]
    return parts[0]


def sum_everywhere(value):
    value = exchange_sum(value, "col", (1,))
    value = exchange_sum(value, "col", (2, 4, 6))
    value = exchange_sum(value, "row", (8, 16, 24))
    value = exchange_sum(value, "row", (1, 2, 3))
    return exchange_sum(value, "row", (4,))


def body(acts, out_grad, lengths):
    n_row = lax.axis_size("row")
    row_idx = lax.axis_index("row")
    own_rows = out_grad.shape[0]
    tokens = own_rows * n_row
    seqs = lengths.shape[0]
    seq_len = tokens // seqs
    positions = row_idx * own_rows + jnp.arange(own_rows, dtype=jnp.int32)
    seq_of = positions // seq_len
    limit = jnp.sum(
        jnp.where(
            seq_of[:, None] == jnp.arange(seqs, dtype=jnp.int32)[None, :], lengths[None, :], 0
        ),
        axis=1,
    )
    live = positions % seq_len < limit
    own_grads = jnp.where(live[:, None], out_grad, jnp.zeros_like(out_grad))
    grads = lax.all_gather(own_grads, "row", axis=0, tiled=True)
    act_full = lax.all_gather(acts, "col", axis=0, tiled=True)
    products = []
    sums = []
    for seq in range(seqs):
        act_rows = act_full[seq * seq_len : (seq + 1) * seq_len]
        grad_rows = grads[seq * seq_len : (seq + 1) * seq_len]
        product = lax.dot_general(
            act_rows, grad_rows, (((0,), (0,)), ((), ())), preferred_element_type=jnp.float32
        )
        products.append(product)
        sums.append(jnp.sum(product * product))
    squares = sum_everywhere(jnp.stack(sums))
    norms = jnp.sqrt(squares / (float(FF) * float(D) * float(seq_len)))
    scale = 1.0 / (norms + 0.1)
    total = scale[0] * products[0]
    for seq in range(1, seqs):
        total = total + scale[seq] * products[seq]
    weight_grad = (total / jnp.sqrt(jnp.float32(tokens))).astype(jnp.bfloat16)
    return (weight_grad, norms)


def solution(mesh):
    placed = (P("col", "row"), P("row", "col"), P())
    return jax.shard_map(
        body, mesh=mesh, in_specs=placed, out_specs=(P("row", "col"), P()), check_vma=False
    )
```

profile of v0, /device:TPU:8, one launch (start us, length us, event | category | flops | bytes accessed | tf_op | source)
XLA Modules:
  0.0 299.2 jit_solution(15958608026676265516)
XLA Ops:
  7.2 0.0 all-gather.5.cloned.1.call-start
  7.2 0.7 all-gather.5.cloned.1.call-update
  7.9 0.0 all-gather.3.cloned.1.call-start
  8.0 0.7 select_reduce_fusion
  8.7 1.8 broadcast_select_fusion
  10.6 0.0 all-gather.3.cloned.1.call-update
  10.6 65.3 %all-gather.5.cloned.1.call-done = bf16[6144,896]{1,0:T(8,128)(2,1)} async-done(((bf16[768,896]{1,0:T(8,128)(2,1)}), bf16[6144,896]{1,0:T(8,128)(2,1)}) %all-gather.5.cloned.1.call-update) | async-done | bytes 11010064 | tf_op jit(solution)/shard_map/all_gather | solution.py:46
  75.9 121.2 %all-gather.3.cloned.1.call-done = bf16[6144,1024]{1,0:T(8,128)(2,1)} async-done(((bf16[192,1024]{1,0:T(8,128)(2,1)}), bf16[6144,1024]{1,0:T(8,128)(2,1)}) %all-gather.3.cloned.1.call-update) | async-done | bytes 12582928 | tf_op jit(solution)/shard_map/all_gather | solution.py:45
  197.1 0.0 slice-start
  197.1 0.0 slice-start.1
  197.1 0.0 copy-start
  197.1 6.3 %multiply_reduce_fusion = (f32[]{:T(128)}, f32[1024,896]{1,0:T(8,128)}) fusion(bf16[6144,896]{1,0:T(8,128)(2,1)} %all-gather.5.cloned.1.call-done, bf16[6144,1024]{1,0:T(8,128)(2,1)} %all-gather.3.cloned.1.call-done), kind=kOutput, calls=%fused_computation.1 | convolution fusion | flops 1411121152 | bytes 6619140 | tf_op jit(solution)/shard_map/dot_general | solution.py:52
  203.3 0.0 slice-start.2
  203.3 7.0 %multiply_reduce_fusion.1 = (f32[]{:T(128)}, f32[1024,896]{1,0:T(8,128)}) fusion(bf16[6144,896]{1,0:T(8,128)(2,1)} %all-gather.5.cloned.1.call-done, bf16[6144,1024]{1,0:T(8,128)(2,1)} %all-gather.3.cloned.1.call-done), kind=kOutput, calls=%fused_computation.2 | convolution fusion | flops 1411121152 | bytes 6619140 | tf_op jit(solution)/shard_map/dot_general | solution.py:52
  210.4 0.0 slice-done
  210.4 0.0 slice-done.1
  210.4 0.0 copy-done
  210.4 0.0 slice-done.2
  210.4 4.3 %multiply_reduce_fusion.2 = (f32[]{:T(128)}, f32[1024,896]{1,0:T(8,128)}) fusion(bf16[6144,896]{1,0:T(8,128)(2,1)S(1)} %copy-done, bf16[6144,1024]{1,0:T(8,128)(2,1)S(1)} %bitcast.19), kind=kOutput, calls=%fused_computation.3 | convolution fusion | flops 1411121152 | bytes 6619140 | tf_op jit(solution)/shard_map/dot_general | solution.py:52
  214.7 4.3 %multiply_reduce_fusion.3 = (f32[]{:T(128)}, f32[1024,896]{1,0:T(8,128)}) fusion(bf16[6144,896]{1,0:T(8,128)(2,1)S(1)} %copy-done, bf16[6144,1024]{1,0:T(8,128)(2,1)S(1)} %bitcast.19), kind=kOutput, calls=%fused_computation.4 | convolution fusion | flops 1411121152 | bytes 6619140 | tf_op jit(solution)/shard_map/dot_general | solution.py:52
  219.0 4.4 %multiply_reduce_fusion.4 = (f32[]{:T(128)}, f32[1024,896]{1,0:T(8,128)}) fusion(bf16[6144,896]{1,0:T(8,128)(2,1)S(1)} %copy-done, bf16[6144,1024]{1,0:T(8,128)(2,1)S(1)} %bitcast.19), kind=kOutput, calls=%fused_computation.5 | convolution fusion | flops 1411121152 | bytes 6619140 | tf_op jit(solution)/shard_map/dot_general | solution.py:52
  223.4 4.4 %multiply_reduce_fusion.5 = (f32[]{:T(128)}, f32[1024,896]{1,0:T(8,128)}) fusion(bf16[6144,896]{1,0:T(8,128)(2,1)S(1)} %copy-done, bf16[6144,1024]{1,0:T(8,128)(2,1)S(1)} %bitcast.19), kind=kOutput, calls=%fused_computation.6 | convolution fusion | flops 1411121152 | bytes 6619140 | tf_op jit(solution)/shard_map/dot_general | solution.py:52
  227.8 4.5 %multiply_reduce_fusion.6 = (f32[]{:T(128)}, f32[1024,896]{1,0:T(8,128)}) fusion(bf16[6144,896]{1,0:T(8,128)(2,1)S(1)} %copy-done, bf16[6144,1024]{1,0:T(8,128)(2,1)S(1)} %bitcast.19), kind=kOutput, calls=%fused_computation.7 | convolution fusion | flops 1411121152 | bytes 6619140 | tf_op jit(solution)/shard_map/dot_general | solution.py:52
  232.3 4.2 %multiply_reduce_fusion.7 = (f32[]{:T(128)}, f32[1024,896]{1,0:T(8,128)}) fusion(bf16[6144,896]{1,0:T(8,128)(2,1)S(1)} %copy-done, bf16[6144,1024]{1,0:T(8,128)(2,1)S(1)} %bitcast.19), kind=kOutput, calls=%fused_computation.8 | convolution fusion | flops 1411121152 | bytes 6619140 | tf_op jit(solution)/shard_map/dot_general | solution.py:52
  236.6 5.1 %stack.35 = f32[8]{0:T(128)S(1)} concatenate(f32[1]{0:T(128)} %bitcast, f32[1]{0:T(128)} %bitcast.1, f32[1]{0:T(128)} %bitcast.2, f32[1]{0:T(128)} %bitcast.3, f32[1]{0:T(128)} %bitcast.4, f32[1]{0:T(128)} %bitcast.5, f32[1]{0:T(128)} %bitcast.6, f32[1]{0:T(128)} %bitcast.7), dimensions={0} | concatenate | bytes 64 | tf_op jit(solution)/shard_map/stack | solution.py:57
  241.7 0.0 collective-permute-start
  241.8 1.1 collective-permute-done
  242.9 2.7 collective-permute-start.3
  245.6 0.8 collective-permute-start.2
  246.4 0.6 collective-permute-start.1
  247.0 0.7 collective-permute-done.3
  247.7 3.0 collective-permute-done.2
  250.7 0.0 collective-permute-done.1
  250.7 1.3 collective-permute-start.6
  252.0 2.7 collective-permute-start.5
  254.6 0.2 collective-permute-start.4
  254.9 0.0 collective-permute-done.6
  254.9 2.2 collective-permute-done.5
  257.0 1.2 collective-permute-done.4
  258.2 3.0 collective-permute-start.9
  261.2 0.0 collective-permute-start.8
  261.2 1.4 collective-permute-start.7
  262.6 1.0 collective-permute-done.9
  263.6 2.1 collective-permute-done.8
  265.7 0.0 collective-permute-done.7
  265.7 2.0 collective-permute-start.10
  267.7 5.5 %collective-permute-done.10 = f32[8]{0:T(128)S(1)} collective-permute-done((f32[8]{0:T(128)S(1)}, f32[8]{0:T(128)S(1)}, u32[]{:S(2)}, u32[]{:S(2)}) %collective-permute-start.10) | collective-permute-done | bytes 64 | tf_op jit(solution)/shard_map/ppermute | solution.py:14
  273.2 0.5 add_divide_fusion
  273.8 0.7 fusion.28
  274.4 15.5 %fusion = bf16[896,1024]{0,1:T(8,128)(2,1)S(1)} fusion(f32[1024,896]{1,0:T(8,128)} %get-tuple-element.31, f32[]{:T(128)} %bitcast.15, f32[1024,896]{1,0:T(8,128)} %get-tuple-element.29, f32[]{:T(128)} %bitcast.14, f32[1024,896]{1,0:T(8,128)} %get-tuple-element.27, f32[]{:T(128)} %bitcast.13, f32[1024,896]{1,0:T(8,128)} %get-tuple-element.25, f32[]{:T(128)} %bitcast.12, ...), kind=kLoop, calls=%fused_computation.9 | loop fusion | flops 15597568 | bytes 31195168 | tf_op jit(solution)/shard_map/convert_element_type | solution.py:63
  289.9 2.4 copy.6
  (7 shorter events, 0.1 us)
Async XLA Ops:
  7.2 68.7 %all-gather.5.cloned.1.call-start = ((), (), s32[]{:S(2)}) async-start(), calls=%async_computation.1 | async-start | bytes 12386304 | tf_op jit(solution)/shard_map/all_gather | solution.py:46
  7.9 189.2 %all-gather.3.cloned.1.call-start = ((), (), s32[]{:S(2)}) async-start(), calls=%async_computation | async-start | bytes 12976128 | tf_op jit(solution)/shard_map/all_gather | solution.py:45
  197.1 13.3 %slice-start = ((s8[12582912]{0:T(1024)(128)(4,1)}), s8[4194304]{0:T(1024)(128)(4,1)S(1)}, s32[]{:S(2)}) async-start(s8[12582912]{0:T(1024)(128)(4,1)} %bitcast.18), calls=%async_computation.2 | async-start | bytes 8388608
  197.1 13.3 %slice-start.1 = ((s8[12582912]{0:T(1024)(128)(4,1)}), s8[4194304]{0:T(1024)(128)(4,1)S(1)}, s32[]{:S(2)}) async-start(s8[12582912]{0:T(1024)(128)(4,1)} %bitcast.18), calls=%async_computation.3 | async-start | bytes 8388608
  197.1 13.3 %copy-start = (bf16[6144,896]{1,0:T(8,128)(2,1)S(1)}, bf16[6144,896]{1,0:T(8,128)(2,1)}, u32[]{:S(2)}) copy-start(bf16[6144,896]{1,0:T(8,128)(2,1)} %all-gather.5.cloned.1.call-done) | copy-start | bytes 33030148
  203.3 7.1 %slice-start.2 = ((s8[12582912]{0:T(1024)(128)(4,1)}), s8[4194304]{0:T(1024)(128)(4,1)S(1)}, s32[]{:S(2)}) async-start(s8[12582912]{0:T(1024)(128)(4,1)} %bitcast.18), calls=%async_computation.4 | async-start | bytes 8388608
  241.7 1.2 collective-permute-start
  242.9 4.8 %collective-permute-start.3 = (f32[8]{0:T(128)S(1)}, f32[8]{0:T(128)S(1)}, u32[]{:S(2)}, u32[]{:S(2)}) collective-permute-start(f32[8]{0:T(128)S(1)} %add.93), channel_id=1, source_target_pairs={{0,6},{1,7},{2,4},{3,5},{4,2},{5,3},{6,0},{7,1},{8,14},{9,15},{10,... | collective-permute-start | bytes 104 | tf_op jit(solution)/shard_map/ppermute | solution.py:14
  245.6 5.1 %collective-permute-start.2 = (f32[8]{0:T(128)S(1)}, f32[8]{0:T(128)S(1)}, u32[]{:S(2)}, u32[]{:S(2)}) collective-permute-start(f32[8]{0:T(128)S(1)} %add.93), channel_id=1, source_target_pairs={{0,4},{1,5},{2,6},{3,7},{4,0},{5,1},{6,2},{7,3},{8,12},{9,13},{10,... | collective-permute-start | bytes 104 | tf_op jit(solution)/shard_map/ppermute | solution.py:14
  246.4 4.2 %collective-permute-start.1 = (f32[8]{0:T(128)S(1)}, f32[8]{0:T(128)S(1)}, u32[]{:S(2)}, u32[]{:S(2)}) collective-permute-start(f32[8]{0:T(128)S(1)} %add.93), channel_id=1, source_target_pairs={{0,2},{1,3},{2,0},{3,1},{4,6},{5,7},{6,4},{7,5},{8,10},{9,11},{10,... | collective-permute-start | bytes 104 | tf_op jit(solution)/shard_map/ppermute | solution.py:14
  250.7 4.2 %collective-permute-start.6 = (f32[8]{0:T(128)S(1)}, f32[8]{0:T(128)S(1)}, u32[]{:S(2)}, u32[]{:S(2)}) collective-permute-start(f32[8]{0:T(128)S(1)} %add_add_fusion.2), channel_id=1, source_target_pairs={{0,192},{8,200},{16,208},{24,216},{32,224},{40,232},{48,240},{56,2... | collective-permute-start | bytes 104 | tf_op jit(solution)/shard_map/ppermute | solution.py:14
  252.0 5.1 %collective-permute-start.5 = (f32[8]{0:T(128)S(1)}, f32[8]{0:T(128)S(1)}, u32[]{:S(2)}, u32[]{:S(2)}) collective-permute-start(f32[8]{0:T(128)S(1)} %add_add_fusion.2), channel_id=1, source_target_pairs={{0,128},{8,136},{16,144},{24,152},{32,160},{40,168},{48,176},{56,1... | collective-permute-start | bytes 104 | tf_op jit(solution)/shard_map/ppermute | solution.py:14
  254.6 3.6 %collective-permute-start.4 = (f32[8]{0:T(128)S(1)}, f32[8]{0:T(128)S(1)}, u32[]{:S(2)}, u32[]{:S(2)}) collective-permute-start(f32[8]{0:T(128)S(1)} %add_add_fusion.2), channel_id=1, source_target_pairs={{0,64},{8,72},{16,80},{24,88},{32,96},{40,104},{48,112},{56,120},{... | collective-permute-start | bytes 104 | tf_op jit(solution)/shard_map/ppermute | solution.py:14
  258.2 5.4 %collective-permute-start.9 = (f32[8]{0:T(128)S(1)}, f32[8]{0:T(128)S(1)}, u32[]{:S(2)}, u32[]{:S(2)}) collective-permute-start(f32[8]{0:T(128)S(1)} %add_add_fusion.1), channel_id=1, source_target_pairs={{0,24},{8,16},{16,8},{24,0},{32,56},{40,48},{48,40},{56,32},{64,88... | collective-permute-start | bytes 104 | tf_op jit(solution)/shard_map/ppermute | solution.py:14
  261.2 4.5 %collective-permute-start.8 = (f32[8]{0:T(128)S(1)}, f32[8]{0:T(128)S(1)}, u32[]{:S(2)}, u32[]{:S(2)}) collective-permute-start(f32[8]{0:T(128)S(1)} %add_add_fusion.1), channel_id=1, source_target_pairs={{0,16},{8,24},{16,0},{24,8},{32,48},{40,56},{48,32},{56,40},{64,80... | collective-permute-start | bytes 104 | tf_op jit(solution)/shard_map/ppermute | solution.py:14
  261.2 4.5 %collective-permute-start.7 = (f32[8]{0:T(128)S(1)}, f32[8]{0:T(128)S(1)}, u32[]{:S(2)}, u32[]{:S(2)}) collective-permute-start(f32[8]{0:T(128)S(1)} %add_add_fusion.1), channel_id=1, source_target_pairs={{0,8},{8,0},{16,24},{24,16},{32,40},{40,32},{48,56},{56,48},{64,72... | collective-permute-start | bytes 104 | tf_op jit(solution)/shard_map/ppermute | solution.py:14
  265.7 7.6 %collective-permute-start.10 = (f32[8]{0:T(128)S(1)}, f32[8]{0:T(128)S(1)}, u32[]{:S(2)}, u32[]{:S(2)}) collective-permute-start(f32[8]{0:T(128)S(1)} %add_add_fusion), channel_id=1, source_target_pairs={{0,32},{8,40},{16,48},{24,56},{32,0},{40,8},{48,16},{56,24},{64,96... | collective-permute-start | bytes 104 | tf_op jit(solution)/shard_map/ppermute | solution.py:14
Sparse Core Ops, SparseCore 0:
  9.8 66.0 all-gather.4
  79.1 117.9 all-gather.2
where the time goes:
time: 299 us
  waiting for transfers between devices  204 us (68%)
  matrix products  39.5 us (13%)
  other arithmetic  18.6 us (6%)
  starting transfers between devices  14.8 us (5%)
  between operations  14.1 us (5%)
  local copies, waits for them, and re-layouts  8.23 us (3%)
    all_gather x1, waiting for transfers between devices, body(): grads = lax.all_gather(own_grads, 'row', axis=0, tiled=True)  121 us
    all_gather x1, waiting for transfers between devices, body(): act_full = lax.all_gather(acts, 'col', axis=0, tiled=True)  65.3 us
    dot_general x8, matrix products, body(): lax.dot_general(act_rows, grad_rows, (((0,), (0,)), ((), ())), preferred_...  39.5 us
    ppermute x11, waiting for transfers between devices, exchange_sum(): lax.ppermute(value, axis, [(i, i ^ shift) for i in range(size)])  16.8 us
    convert_element_type x1, other arithmetic, body(): weight_grad = (total / jnp.sqrt(jnp.float32(tokens))).astype(jnp.bfloat16)  15.5 us
    ppermute x11, starting transfers between devices, exchange_sum(): lax.ppermute(value, axis, [(i, i ^ shift) for i in range(size)])  14.7 us
  transfers between devices with their start and end apart: 13, of which 10 were waited for; matrix products, arithmetic and copies ran while one was open for 1% of the time, Pallas kernels for 0%

commit v1 on v0

--- a/solution.py
+++ b/solution.py
@@ -1,3 +1,4 @@
+import functools
 import jax
 import jax.numpy as jnp
 from jax import lax
@@ -5,6 +6,31 @@
 
 FF = 28672
 D = 8192
+
+
+def find_weights(array_here, row_dim):
+    array_here = jnp.moveaxis(array_here, 0, row_dim)
+    t1 = array_here.shape
+    return array_here.reshape(*t1[:row_dim], t1[row_dim] * t1[row_dim + 1], *t1[row_dim + 2 :])
+
+
+def build_the_figure(x0, mesh_dim, axis_no):
+    wide_n = lax.axis_size(mesh_dim)
+    heap = [(num, (num + 1) % wide_n) for num in range(wide_n)]
+    stack_in = [(b, s) for s, b in heap]
+    y_new, field_out = ([], [])
+    for j in range(wide_n - 1):
+        if j % 2 == 0:
+            y_new.append(lax.ppermute(y_new[-1] if y_new else x0, mesh_dim, heap))
+        else:
+            field_out.append(lax.ppermute(field_out[-1] if field_out else x0, mesh_dim, stack_in))
+    carry_in = jnp.stack([*y_new[::-1], x0, *field_out], axis=0)
+    part_next = lax.axis_index(mesh_dim) - len(y_new)
+    carry_in = carry_in[(jnp.arange(wide_n) - part_next) % wide_n]
+    return find_weights(carry_in, axis_no)
+
+
+_replace_shards = functools.partial(build_the_figure, mesh_dim="col", axis_no=0)
 
 
 def exchange_sum(value, axis, shifts):
@@ -43,7 +69,7 @@
     live = positions % seq_len < limit
     own_grads = jnp.where(live[:, None], out_grad, jnp.zeros_like(out_grad))
     grads = lax.all_gather(own_grads, "row", axis=0, tiled=True)
-    act_full = lax.all_gather(acts, "col", axis=0, tiled=True)
+    act_full = _replace_shards(acts)
     products = []
     sums = []
     for seq in range(seqs):

time: 299 us -> 232 us (0.78)
  waiting for transfers between devices: 204 us -> 104 us
  local copies, waits for them, and re-layouts: 8.23 us -> 30.9 us
  starting transfers between devices: 14.8 us -> 23.3 us
    all_gather x1, waiting for transfers between devices: 121 us -> 20.6 us  [body(): grads = lax.all_gather(own_grads, 'row', axis=0, tiled=True)]
    ppermute x0 -> x7, waiting for transfers between devices: none -> 67 us  [the longest x4 66.7 us: build_the_figure(): y_new.append(lax.ppermute(y_new[-1] if y_new else x0, mesh_dim, heap))]
    all_gather x1 -> x0, waiting for transfers between devices: 65.3 us -> none  [body(): act_full = lax.all_gather(acts, 'col', axis=0, tiled=True)]
    unnamed x9 -> x17, local copies, waits for them, and re-layouts: 2.42 us -> 13.6 us
    gather x0 -> x1, local copies, waits for them, and re-layouts: none -> 10.4 us  [build_the_figure(): carry_in = carry_in[(jnp.arange(wide_n) - part_next) % wide_n]]
    ppermute x0 -> x7, starting transfers between devices: none -> 8.51 us  [the longest x3 8.48 us: build_the_figure(): lax.ppermute(field_out[-1] if field_out else x0, mesh_dim, stack_in)]
  transfers between devices with their start and end apart: 13 -> 19, of which waited for: 10 -> 15; matrix products, arithmetic and copies ran while one was open for 1% -> 10% of each run, Pallas kernels for 0% -> 0%
where the time goes in v1:
time: 232 us; the launch traced here: 231 us
  waiting for transfers between devices  104 us (45%)
  matrix products  38.1 us (16%)
  local copies, waits for them, and re-layouts  30.9 us (13%)
  starting transfers between devices  23.3 us (10%)
  other arithmetic  20.7 us (9%)
  between operations  14.1 us (6%)
    ppermute x4, waiting for transfers between devices, build_the_figure(): y_new.append(lax.ppermute(y_new[-1] if y_new else x0, mesh_dim, heap))  66.7 us
    dot_general x8, matrix products, body(): lax.dot_general(act_rows, grad_rows, (((0,), (0,)), ((), ())), preferred_...  38.1 us
    all_gather x1, waiting for transfers between devices, body(): grads = lax.all_gather(own_grads, 'row', axis=0, tiled=True)  20.6 us
    convert_element_type x1, other arithmetic, body(): weight_grad = (total / jnp.sqrt(jnp.float32(tokens))).astype(jnp.bfloat16)  17.5 us
    ppermute x11, waiting for transfers between devices, exchange_sum(): lax.ppermute(value, axis, [(i, i ^ shift) for i in range(size)])  16.8 us
    ppermute x11, starting transfers between devices, exchange_sum(): lax.ppermute(value, axis, [(i, i ^ shift) for i in range(size)])  14.7 us
    unnamed x17, local copies, waits for them, and re-layouts  13.6 us
    gather x1, local copies, waits for them, and re-layouts, build_the_figure(): carry_in = carry_in[(jnp.arange(wide_n) - part_next) % wide_n]  10.4 us
  transfers between devices with their start and end apart: 19, of which 15 were waited for; matrix products, arithmetic and copies ran while one was open for 10% of the time, Pallas kernels for 0%

profile of v1, /device:TPU:8, one launch (start us, length us, event | category | flops | bytes accessed | tf_op | source)
XLA Modules:
  0.0 231.4 jit_solution(12579386456246285696)
XLA Ops:
  7.2 0.0 all-gather.2.cloned.1.call-start
  7.2 0.7 select_reduce_fusion
  8.0 1.9 broadcast_select_fusion
  9.8 0.0 all-gather.2.cloned.1.call-update
  9.9 0.0 collective-permute-start
  9.9 19.1 %collective-permute-done = bf16[768,896]{1,0:T(8,128)(2,1)S(1)} collective-permute-done((bf16[768,896]{1,0:T(8,128)(2,1)}, bf16[768,896]{1,0:T(8,128)(2,1)S(1)}, u32[]{:S(2)}, u32[]{:S(2)}) %collective-permute-start) | collective-permute-done | bytes 1376288 | tf_op jit(solution)/shard_map/ppermute | solution.py:24
  29.0 0.0 collective-permute-start.1
  29.0 3.0 %collective-permute-start.4 = (bf16[768,896]{1,0:T(8,128)(2,1)}, bf16[768,896]{1,0:T(8,128)(2,1)S(1)}, u32[]{:S(2)}, u32[]{:S(2)}) collective-permute-start(bf16[768,896]{1,0:T(8,128)(2,1)} %param.3), channel_id=1, source_target_pairs={{1,0},{2,1},{3,2},{4,3},{5,4},{6,5},{7,6},{0,7},{9,8},{10,9},{11,1... | collective-permute-start | bytes 4128776 | tf_op jit(solution)/shard_map/ppermute | solution.py:26
  32.0 16.0 %collective-permute-done.1 = bf16[768,896]{1,0:T(8,128)(2,1)S(1)} collective-permute-done((bf16[768,896]{1,0:T(8,128)(2,1)S(1)}, bf16[768,896]{1,0:T(8,128)(2,1)S(1)}, u32[]{:S(2)}, u32[]{:S(2)}) %collective-permute-start.1) | collective-permute-done | bytes 1376288 | tf_op jit(solution)/shard_map/ppermute | solution.py:24
  48.0 0.0 collective-permute-start.2
  48.0 0.1 collective-permute-done.4
  48.1 0.9 copy-done.2
  49.1 2.3 collective-permute-start.5
  51.4 15.7 %collective-permute-done.2 = bf16[768,896]{1,0:T(8,128)(2,1)} collective-permute-done((bf16[768,896]{1,0:T(8,128)(2,1)S(1)}, bf16[768,896]{1,0:T(8,128)(2,1)}, u32[]{:S(2)}, u32[]{:S(2)}) %collective-permute-start.2) | collective-permute-done | bytes 1376288 | tf_op jit(solution)/shard_map/ppermute | solution.py:24
  67.0 0.0 collective-permute-start.3
  67.1 0.1 collective-permute-done.5
  67.2 3.2 %collective-permute-start.6 = (bf16[768,896]{1,0:T(8,128)(2,1)}, bf16[768,896]{1,0:T(8,128)(2,1)S(1)}, u32[]{:S(2)}, u32[]{:S(2)}) collective-permute-start(bf16[768,896]{1,0:T(8,128)(2,1)} %collective-permute-done.5), channel_id=1, source_target_pairs={{1,0},{2,1},{3,2},{4,3},{5,4},{6,5},{7,6},{0,7},{9,8},{10,9},{11,1... | collective-permute-start | bytes 4128776 | tf_op jit(solution)/shard_map/ppermute | solution.py:26
  70.4 15.9 %collective-permute-done.3 = bf16[768,896]{1,0:T(8,128)(2,1)} collective-permute-done((bf16[768,896]{1,0:T(8,128)(2,1)}, bf16[768,896]{1,0:T(8,128)(2,1)}, u32[]{:S(2)}, u32[]{:S(2)}) %collective-permute-start.3) | collective-permute-done | bytes 1376288 | tf_op jit(solution)/shard_map/ppermute | solution.py:24
  86.3 2.6 %bitcast_dynamic-update-slice_fusion.7 = bf16[8,768,896]{2,1,0:T(8,128)(2,1)} fusion(bf16[768,896]{1,0:T(8,128)(2,1)} %collective-permute-done.3), kind=kLoop, calls=%fused_computation.41 | loop fusion | bytes 2752512
  88.9 2.6 %bitcast_dynamic-update-slice_fusion.6 = bf16[8,768,896]{2,1,0:T(8,128)(2,1)} fusion(bf16[8,768,896]{2,1,0:T(8,128)(2,1)} %bitcast_dynamic-update-slice_fusion.7, bf16[768,896]{1,0:T(8,128)(2,1)} %collective-permute-done.2), kind=kLoop, calls=%fused_computation.40 | loop fusion | bytes 2752512
  91.6 1.2 bitcast_dynamic-update-slice_fusion.5
  92.8 1.2 bitcast_dynamic-update-slice_fusion.4
  94.0 1.2 bitcast_dynamic-update-slice_fusion.3
  95.2 1.2 bitcast_dynamic-update-slice_fusion.2
  96.4 2.6 %bitcast_dynamic-update-slice_fusion.1 = bf16[8,768,896]{2,1,0:T(8,128)(2,1)} fusion(bf16[8,768,896]{2,1,0:T(8,128)(2,1)} %bitcast_dynamic-update-slice_fusion.2, bf16[768,896]{1,0:T(8,128)(2,1)} %collective-permute-done.5), kind=kLoop, calls=%fused_computation.35 | loop fusion | bytes 2752512
  98.9 0.0 collective-permute-done.6
  98.9 1.2 bitcast_dynamic-update-slice_fusion
  100.2 10.4 %gather_fusion = bf16[8,768,896]{2,1,0:T(8,128)(2,1)} fusion(bf16[8,768,896]{2,1,0:T(8,128)(2,1)} %bitcast_dynamic-update-slice_fusion, s32[1024]{0:T(1024)S(1)} %pad_clamp_fusion), kind=kCustom, calls=%fused_computation | custom fusion | bytes 22020128 | tf_op jit(solution)/shard_map/gather | solution.py:29
  110.5 20.6 %all-gather.2.cloned.1.call-done = bf16[6144,1024]{1,0:T(8,128)(2,1)} async-done(((bf16[192,1024]{1,0:T(8,128)(2,1)}), bf16[6144,1024]{1,0:T(8,128)(2,1)}) %all-gather.2.cloned.1.call-update) | async-done | bytes 12582928 | tf_op jit(solution)/shard_map/all_gather | solution.py:71
  131.1 6.0 %multiply_reduce_fusion.1 = (f32[]{:T(128)}, f32[896,1024]{1,0:T(8,128)}) fusion(bf16[6144,1024]{1,0:T(8,128)(2,1)} %all-gather.2.cloned.1.call-done, bf16[8,768,896]{2,1,0:T(8,128)(2,1)} %gather_fusion), kind=kOutput, calls=%fused_computation.3 | convolution fusion | flops 1411121152 | bytes 6619140 | tf_op jit(solution)/shard_map/dot_general | solution.py:78
  137.1 0.0 copy-done
  137.1 5.8 %multiply_reduce_fusion.2 = (f32[]{:T(128)}, f32[896,1024]{1,0:T(8,128)}) fusion(bf16[6144,1024]{1,0:T(8,128)(2,1)} %all-gather.2.cloned.1.call-done, bf16[8,768,896]{2,1,0:T(8,128)(2,1)S(1)} %copy-done), kind=kOutput, calls=%fused_computation.4 | convolution fusion | flops 1411121152 | bytes 6619140 | tf_op jit(solution)/shard_map/dot_general | solution.py:78
  142.8 5.6 %multiply_reduce_fusion.3 = (f32[]{:T(128)}, f32[896,1024]{1,0:T(8,128)}) fusion(bf16[6144,1024]{1,0:T(8,128)(2,1)} %all-gather.2.cloned.1.call-done, bf16[8,768,896]{2,1,0:T(8,128)(2,1)S(1)} %copy-done), kind=kOutput, calls=%fused_computation.5 | convolution fusion | flops 1411121152 | bytes 6619140 | tf_op jit(solution)/shard_map/dot_general | solution.py:78
  148.4 4.0 %multiply_reduce_fusion.4 = (f32[]{:T(128)}, f32[896,1024]{1,0:T(8,128)}) fusion(bf16[6144,1024]{1,0:T(8,128)(2,1)S(1)} %copy-done.4, bf16[8,768,896]{2,1,0:T(8,128)(2,1)S(1)} %copy-done), kind=kOutput, calls=%fused_computation.6 | convolution fusion | flops 1411121152 | bytes 6619140 | tf_op jit(solution)/shard_map/dot_general | solution.py:78
  152.5 4.1 %multiply_reduce_fusion.5 = (f32[]{:T(128)}, f32[896,1024]{1,0:T(8,128)}) fusion(bf16[6144,1024]{1,0:T(8,128)(2,1)S(1)} %copy-done.4, bf16[8,768,896]{2,1,0:T(8,128)(2,1)S(1)} %copy-done), kind=kOutput, calls=%fused_computation.7 | convolution fusion | flops 1411121152 | bytes 6619140 | tf_op jit(solution)/shard_map/dot_general | solution.py:78
  156.6 4.2 %multiply_reduce_fusion.6 = (f32[]{:T(128)}, f32[896,1024]{1,0:T(8,128)}) fusion(bf16[6144,1024]{1,0:T(8,128)(2,1)S(1)} %copy-done.4, bf16[8,768,896]{2,1,0:T(8,128)(2,1)S(1)} %copy-done), kind=kOutput, calls=%fused_computation.8 | convolution fusion | flops 1411121152 | bytes 6619140 | tf_op jit(solution)/shard_map/dot_general | solution.py:78
  160.7 4.2 %multiply_reduce_fusion.7 = (f32[]{:T(128)}, f32[896,1024]{1,0:T(8,128)}) fusion(bf16[6144,1024]{1,0:T(8,128)(2,1)S(1)} %copy-done.4, bf16[8,768,896]{2,1,0:T(8,128)(2,1)S(1)} %copy-done), kind=kOutput, calls=%fused_computation.9 | convolution fusion | flops 1411121152 | bytes 6619140 | tf_op jit(solution)/shard_map/dot_general | solution.py:78
  164.9 4.4 %multiply_reduce_fusion = (f32[]{:T(128)}, f32[896,1024]{1,0:T(8,128)}) fusion(bf16[6144,1024]{1,0:T(8,128)(2,1)S(1)} %copy-done.4, bf16[8,768,896]{2,1,0:T(8,128)(2,1)S(1)} %copy-done), kind=kOutput, calls=%fused_computation.2 | convolution fusion | flops 1411121152 | bytes 6619140 | tf_op jit(solution)/shard_map/dot_general | solution.py:78
  169.2 5.1 %stack.71 = f32[8]{0:T(128)S(1)} concatenate(f32[1]{0:T(128)} %bitcast.10, f32[1]{0:T(128)} %bitcast.12, f32[1]{0:T(128)} %bitcast.14, f32[1]{0:T(128)} %bitcast.16, f32[1]{0:T(128)} %bitcast.18, f32[1]{0:T(128)} %bitcast.20, f32[1]{0:T(128)} %bitcast.22, f32[1]{0:T(128)} %bitcast.24), dimensions={0} | concatenate | bytes 64 | tf_op jit(solution)/shard_map/stack | solution.py:83
  174.3 0.0 collective-permute-start.7
  174.4 1.1 collective-permute-done.7
  175.5 2.7 %collective-permute-start.10 = (f32[8]{0:T(128)S(1)}, f32[8]{0:T(128)S(1)}, u32[]{:S(2)}, u32[]{:S(2)}) collective-permute-start(f32[8]{0:T(128)S(1)} %add.114), channel_id=1, source_target_pairs={{0,6},{1,7},{2,4},{3,5},{4,2},{5,3},{6,0},{7,1},{8,14},{9,15},{10,... | collective-permute-start | bytes 104 | tf_op jit(solution)/shard_map/ppermute | solution.py:40
  178.2 0.8 collective-permute-start.9
  179.1 0.6 collective-permute-start.8
  179.6 0.7 collective-permute-done.10
  180.3 3.0 %collective-permute-done.9 = f32[8]{0:T(128)S(1)} collective-permute-done((f32[8]{0:T(128)S(1)}, f32[8]{0:T(128)S(1)}, u32[]{:S(2)}, u32[]{:S(2)}) %collective-permute-start.9) | collective-permute-done | bytes 64 | tf_op jit(solution)/shard_map/ppermute | solution.py:40
  183.3 0.0 collective-permute-done.8
  183.3 1.3 collective-permute-start.13
  184.6 2.7 %collective-permute-start.12 = (f32[8]{0:T(128)S(1)}, f32[8]{0:T(128)S(1)}, u32[]{:S(2)}, u32[]{:S(2)}) collective-permute-start(f32[8]{0:T(128)S(1)} %add_add_fusion.2), channel_id=1, source_target_pairs={{0,128},{8,136},{16,144},{24,152},{32,160},{40,168},{48,176},{56,1... | collective-permute-start | bytes 104 | tf_op jit(solution)/shard_map/ppermute | solution.py:40
  187.3 0.2 collective-permute-start.11
  187.5 0.0 collective-permute-done.13
  187.5 2.2 collective-permute-done.12
  189.6 1.2 collective-permute-done.11
  190.8 3.0 %collective-permute-start.16 = (f32[8]{0:T(128)S(1)}, f32[8]{0:T(128)S(1)}, u32[]{:S(2)}, u32[]{:S(2)}) collective-permute-start(f32[8]{0:T(128)S(1)} %add_add_fusion.1), channel_id=1, source_target_pairs={{0,24},{8,16},{16,8},{24,0},{32,56},{40,48},{48,40},{56,32},{64,88... | collective-permute-start | bytes 104 | tf_op jit(solution)/shard_map/ppermute | solution.py:40
  193.8 0.0 collective-permute-start.15
  193.8 1.4 collective-permute-start.14
  195.2 1.0 collective-permute-done.16
  196.2 2.1 collective-permute-done.15
  198.3 0.0 collective-permute-done.14
  198.3 2.0 collective-permute-start.17
  200.3 5.5 %collective-permute-done.17 = f32[8]{0:T(128)S(1)} collective-permute-done((f32[8]{0:T(128)S(1)}, f32[8]{0:T(128)S(1)}, u32[]{:S(2)}, u32[]{:S(2)}) %collective-permute-start.17) | collective-permute-done | bytes 64 | tf_op jit(solution)/shard_map/ppermute | solution.py:40
  205.9 0.5 add_divide_fusion
  206.4 0.7 fusion.21
  207.1 17.5 %multiply_convert_fusion = bf16[896,1024]{1,0:T(8,128)(2,1)} fusion(f32[896,1024]{1,0:T(8,128)} %get-tuple-element.27, f32[896,1024]{1,0:T(8,128)} %get-tuple-element.25, f32[896,1024]{1,0:T(8,128)} %get-tuple-element.23, f32[896,1024]{1,0:T(8,128)} %get-tuple-element.21, f32[896,1024]{1,0:T(8,128)} %get-tuple-element.19, f32[896,1024]{1,0:T(8,128)} %get-tuple-element.17, ...), kind=kLoop, calls=%fused_computation.1 | loop fusion | flops 15597568 | bytes 31195168 | tf_op jit(solution)/shard_map/convert_element_type | solution.py:89
  (16 shorter events, 0.1 us)
Async XLA Ops:
  7.2 123.9 %all-gather.2.cloned.1.call-start = ((), (), s32[]{:S(2)}) async-start(), calls=%async_computation | async-start | bytes 12976128 | tf_op jit(solution)/shard_map/all_gather | solution.py:71
  9.9 19.2 %collective-permute-start = (bf16[768,896]{1,0:T(8,128)(2,1)}, bf16[768,896]{1,0:T(8,128)(2,1)S(1)}, u32[]{:S(2)}, u32[]{:S(2)}) collective-permute-start(bf16[768,896]{1,0:T(8,128)(2,1)} %param.3), channel_id=1, source_target_pairs={{0,1},{1,2},{2,3},{3,4},{4,5},{5,6},{6,7},{7,0},{8,9},{9,10},{10,1... | collective-permute-start | bytes 4128776 | tf_op jit(solution)/shard_map/ppermute | solution.py:24
  29.0 18.9 %collective-permute-start.1 = (bf16[768,896]{1,0:T(8,128)(2,1)S(1)}, bf16[768,896]{1,0:T(8,128)(2,1)S(1)}, u32[]{:S(2)}, u32[]{:S(2)}) collective-permute-start(bf16[768,896]{1,0:T(8,128)(2,1)S(1)} %collective-permute-done), channel_id=1, source_target_pairs={{0,1},{1,2},{2,3},{3,4},{4,5},{5,6},{6,7},{7,0},{8,9},{9,10},{10,1... | collective-permute-start | bytes 4128776 | tf_op jit(solution)/shard_map/ppermute | solution.py:24
  29.0 19.1 %collective-permute-start.4 = (bf16[768,896]{1,0:T(8,128)(2,1)}, bf16[768,896]{1,0:T(8,128)(2,1)S(1)}, u32[]{:S(2)}, u32[]{:S(2)}) collective-permute-start(bf16[768,896]{1,0:T(8,128)(2,1)} %param.3), channel_id=1, source_target_pairs={{1,0},{2,1},{3,2},{4,3},{5,4},{6,5},{7,6},{0,7},{9,8},{10,9},{11,1... | collective-permute-start | bytes 4128776 | tf_op jit(solution)/shard_map/ppermute | solution.py:26
  48.0 1.1 copy-start.2
  48.0 19.1 %collective-permute-start.2 = (bf16[768,896]{1,0:T(8,128)(2,1)S(1)}, bf16[768,896]{1,0:T(8,128)(2,1)}, u32[]{:S(2)}, u32[]{:S(2)}) collective-permute-start(bf16[768,896]{1,0:T(8,128)(2,1)S(1)} %collective-permute-done.1), channel_id=1, source_target_pairs={{0,1},{1,2},{2,3},{3,4},{4,5},{5,6},{6,7},{7,0},{8,9},{9,10},{10,1... | collective-permute-start | bytes 4128776 | tf_op jit(solution)/shard_map/ppermute | solution.py:24
  49.1 18.1 %collective-permute-start.5 = (bf16[768,896]{1,0:T(8,128)(2,1)S(1)}, bf16[768,896]{1,0:T(8,128)(2,1)}, u32[]{:S(2)}, u32[]{:S(2)}) collective-permute-start(bf16[768,896]{1,0:T(8,128)(2,1)S(1)} %collective-permute-done.4), channel_id=1, source_target_pairs={{1,0},{2,1},{3,2},{4,3},{5,4},{6,5},{7,6},{0,7},{9,8},{10,9},{11,1... | collective-permute-start | bytes 4128776 | tf_op jit(solution)/shard_map/ppermute | solution.py:26
  67.0 19.3 %collective-permute-start.3 = (bf16[768,896]{1,0:T(8,128)(2,1)}, bf16[768,896]{1,0:T(8,128)(2,1)}, u32[]{:S(2)}, u32[]{:S(2)}) collective-permute-start(bf16[768,896]{1,0:T(8,128)(2,1)} %collective-permute-done.2), channel_id=1, source_target_pairs={{0,1},{1,2},{2,3},{3,4},{4,5},{5,6},{6,7},{7,0},{8,9},{9,10},{10,1... | collective-permute-start | bytes 4128776 | tf_op jit(solution)/shard_map/ppermute | solution.py:24
  67.0 24.5 %copy-start.3 = (bf16[768,896]{1,0:T(8,128)(2,1)S(1)}, bf16[768,896]{1,0:T(8,128)(2,1)}, u32[]{:S(2)}) copy-start(bf16[768,896]{1,0:T(8,128)(2,1)} %copy-done.2) | copy-start | bytes 4128772
  67.2 31.7 %collective-permute-start.6 = (bf16[768,896]{1,0:T(8,128)(2,1)}, bf16[768,896]{1,0:T(8,128)(2,1)S(1)}, u32[]{:S(2)}, u32[]{:S(2)}) collective-permute-start(bf16[768,896]{1,0:T(8,128)(2,1)} %collective-permute-done.5), channel_id=1, source_target_pairs={{1,0},{2,1},{3,2},{4,3},{5,4},{6,5},{7,6},{0,7},{9,8},{10,9},{11,1... | collective-permute-start | bytes 4128776 | tf_op jit(solution)/shard_map/ppermute | solution.py:26
  88.9 5.1 %copy-start.1 = (bf16[768,896]{1,0:T(8,128)(2,1)S(1)}, bf16[768,896]{1,0:T(8,128)(2,1)}, u32[]{:S(2)}) copy-start(bf16[768,896]{1,0:T(8,128)(2,1)} %param.3) | copy-start | bytes 4128772
  131.1 6.0 %copy-start = (bf16[8,768,896]{2,1,0:T(8,128)(2,1)S(1)}, bf16[8,768,896]{2,1,0:T(8,128)(2,1)}, u32[]{:S(2)}) copy-start(bf16[8,768,896]{2,1,0:T(8,128)(2,1)} %gather_fusion) | copy-start | bytes 33030148
  137.1 11.3 %copy-start.4 = (bf16[6144,1024]{1,0:T(8,128)(2,1)S(1)}, bf16[6144,1024]{1,0:T(8,128)(2,1)}, u32[]{:S(2)}) copy-start(bf16[6144,1024]{1,0:T(8,128)(2,1)} %all-gather.2.cloned.1.call-done) | copy-start | bytes 37748740
  174.3 1.2 collective-permute-start.7
  175.5 4.8 %collective-permute-start.10 = (f32[8]{0:T(128)S(1)}, f32[8]{0:T(128)S(1)}, u32[]{:S(2)}, u32[]{:S(2)}) collective-permute-start(f32[8]{0:T(128)S(1)} %add.114), channel_id=1, source_target_pairs={{0,6},{1,7},{2,4},{3,5},{4,2},{5,3},{6,0},{7,1},{8,14},{9,15},{10,... | collective-permute-start | bytes 104 | tf_op jit(solution)/shard_map/ppermute | solution.py:40
  178.2 5.1 %collective-permute-start.9 = (f32[8]{0:T(128)S(1)}, f32[8]{0:T(128)S(1)}, u32[]{:S(2)}, u32[]{:S(2)}) collective-permute-start(f32[8]{0:T(128)S(1)} %add.114), channel_id=1, source_target_pairs={{0,4},{1,5},{2,6},{3,7},{4,0},{5,1},{6,2},{7,3},{8,12},{9,13},{10,... | collective-permute-start | bytes 104 | tf_op jit(solution)/shard_map/ppermute | solution.py:40
  179.1 4.2 %collective-permute-start.8 = (f32[8]{0:T(128)S(1)}, f32[8]{0:T(128)S(1)}, u32[]{:S(2)}, u32[]{:S(2)}) collective-permute-start(f32[8]{0:T(128)S(1)} %add.114), channel_id=1, source_target_pairs={{0,2},{1,3},{2,0},{3,1},{4,6},{5,7},{6,4},{7,5},{8,10},{9,11},{10,... | collective-permute-start | bytes 104 | tf_op jit(solution)/shard_map/ppermute | solution.py:40
  183.3 4.2 %collective-permute-start.13 = (f32[8]{0:T(128)S(1)}, f32[8]{0:T(128)S(1)}, u32[]{:S(2)}, u32[]{:S(2)}) collective-permute-start(f32[8]{0:T(128)S(1)} %add_add_fusion.2), channel_id=1, source_target_pairs={{0,192},{8,200},{16,208},{24,216},{32,224},{40,232},{48,240},{56,2... | collective-permute-start | bytes 104 | tf_op jit(solution)/shard_map/ppermute | solution.py:40
  184.6 5.1 %collective-permute-start.12 = (f32[8]{0:T(128)S(1)}, f32[8]{0:T(128)S(1)}, u32[]{:S(2)}, u32[]{:S(2)}) collective-permute-start(f32[8]{0:T(128)S(1)} %add_add_fusion.2), channel_id=1, source_target_pairs={{0,128},{8,136},{16,144},{24,152},{32,160},{40,168},{48,176},{56,1... | collective-permute-start | bytes 104 | tf_op jit(solution)/shard_map/ppermute | solution.py:40
  187.3 3.6 %collective-permute-start.11 = (f32[8]{0:T(128)S(1)}, f32[8]{0:T(128)S(1)}, u32[]{:S(2)}, u32[]{:S(2)}) collective-permute-start(f32[8]{0:T(128)S(1)} %add_add_fusion.2), channel_id=1, source_target_pairs={{0,64},{8,72},{16,80},{24,88},{32,96},{40,104},{48,112},{56,120},{... | collective-permute-start | bytes 104 | tf_op jit(solution)/shard_map/ppermute | solution.py:40
  190.8 5.4 %collective-permute-start.16 = (f32[8]{0:T(128)S(1)}, f32[8]{0:T(128)S(1)}, u32[]{:S(2)}, u32[]{:S(2)}) collective-permute-start(f32[8]{0:T(128)S(1)} %add_add_fusion.1), channel_id=1, source_target_pairs={{0,24},{8,16},{16,8},{24,0},{32,56},{40,48},{48,40},{56,32},{64,88... | collective-permute-start | bytes 104 | tf_op jit(solution)/shard_map/ppermute | solution.py:40
  193.8 4.5 %collective-permute-start.15 = (f32[8]{0:T(128)S(1)}, f32[8]{0:T(128)S(1)}, u32[]{:S(2)}, u32[]{:S(2)}) collective-permute-start(f32[8]{0:T(128)S(1)} %add_add_fusion.1), channel_id=1, source_target_pairs={{0,16},{8,24},{16,0},{24,8},{32,48},{40,56},{48,32},{56,40},{64,80... | collective-permute-start | bytes 104 | tf_op jit(solution)/shard_map/ppermute | solution.py:40
  193.8 4.5 %collective-permute-start.14 = (f32[8]{0:T(128)S(1)}, f32[8]{0:T(128)S(1)}, u32[]{:S(2)}, u32[]{:S(2)}) collective-permute-start(f32[8]{0:T(128)S(1)} %add_add_fusion.1), channel_id=1, source_target_pairs={{0,8},{8,0},{16,24},{24,16},{32,40},{40,32},{48,56},{56,48},{64,72... | collective-permute-start | bytes 104 | tf_op jit(solution)/shard_map/ppermute | solution.py:40
  198.3 7.6 %collective-permute-start.17 = (f32[8]{0:T(128)S(1)}, f32[8]{0:T(128)S(1)}, u32[]{:S(2)}, u32[]{:S(2)}) collective-permute-start(f32[8]{0:T(128)S(1)} %add_add_fusion), channel_id=1, source_target_pairs={{0,32},{8,40},{16,48},{24,56},{32,0},{40,8},{48,16},{56,24},{64,96... | collective-permute-start | bytes 104 | tf_op jit(solution)/shard_map/ppermute | solution.py:40
Sparse Core Ops, SparseCore 0:
  10.5 120.4 all-gather.1
